TPU v7x, 256 devices: a whole 4x4x8 slice. The times are simulated.
256 devices in a mesh: coh: 4 (over y), lat: 4 (over x), lon: 16 (over z, core).
Axes of the slice: x: 4, y: 4, z: 8, core: 2. Of those that a mesh axis runs over, the one named last changes fastest.
Arguments:
- saved_period_abundance: bfloat16 [2, 128, 256, 4096], P(None, 'coh', 'lat', 'lon'), may hold values from 0.099609375 to 2
- final_abundance_sensitivity: bfloat16 [128, 256, 4096], P('coh', 'lat', 'lon'), may hold values from -6 to 6
- prey_biomass: float32 [2, 256, 4096], P(None, 'lat', 'lon'), may hold values from 0.2 to 2
- water_heat_field: float32 [2, 256, 4096], P(None, 'lat', 'lon'), may hold values from 10 to 30
- marine_indicator: int32 [256, 4096], P('lat', 'lon'), may hold values 0 or 1
- fishing_pressure: float32 [256, 4096], P('lat', 'lon'), may hold values from 0.1 to 2
- offspring_yield: float32 [256, 4096], P('lat', 'lon'), may hold values from 2 to 20
- death_fraction: float32 [128], P('coh'), may hold values from 0.01 to 0.5
- gear_vulnerability: float32 [128], P('coh'), may hold values from 0.05 to 0.5
- spreading_coefficient: float32 [128], P('coh'), may hold values from 0.02 to 0.12
- directed_drift_rate: float32 [128], P('coh'), may hold values from 0.01 to 0.06
- favoured_thermal_level: float32 [128], P('coh'), may hold values from 12 to 28
- breeding_contribution: float32 [128], P('coh'), may hold values from 0.005 to 0.03
- landing_error_sensitivity: float32 [2048, 2, 128], P(('lat', 'lon'), None, 'coh'), may hold values from -6 to 6
- fleet_east_piece: int32 [2048, 1], P(('lat', 'lon')), may hold values from 0 to 15; in each aligned block of 32 rows (0 to 31, 32 to 63, ...) at most 3 rows name the same one
- fleet_north_piece: int32 [2048], P(('lat', 'lon')), may hold values from 0 to 3
- fleet_area_patch: int32 [2048], P(('lat', 'lon')), may hold values from 0 to 31
- fleet_age_bounds: int32 [2048, 2], P(('lat', 'lon')), may hold values from 0 to 128, as said below
Outputs:
- density_grad: float32 [128, 256, 4096], P('coh', 'lat', 'lon')
- recruit_grad: float32 [256, 4096], P('lat', 'lon')
Inputs may be any that keep to these rules, and one draw needn't show every extreme that they name: `fleet_east_piece`: among the rows of one device, at most 3 name the same longitude tile, and some longitude tile is named by exactly 3 of them. `fleet_age_bounds`: in every row the first entry is below the second.
All inputs are finite; a program needn't handle non-finite values. No bound on the sum of `marine_indicator` on one device may be relied on, other than what follows from the above.
Results may differ from a plain program's by a relative error of at most 0.0003.
Values sent between devices are 32-bit elements; how exact they have to be, the bound alone decides.
A program may use at most 64 MiB of HBM per device.

v0:
```python
import jax
import jax.numpy as jnp
from jax import lax
from jax.sharding import PartitionSpec as P

BY = 16
BX = 32
thermal_tolerance_spread = 4.0
highest = lax.Precision.HIGHEST


def from_root(value, axis, source):
    kept = jnp.where(lax.axis_index(axis) == source, value, 0).astype(value.dtype)
    return lax.psum(kept, axis)


def shifted(block, axis, distance):
    devices = range(lax.axis_size(axis))
    route = [(i - distance, i) for i in devices if i - distance in devices]
    return lax.ppermute(block, axis, route)


def with_halo(x, sides, width):
    for axis, dim in sides:
        devices, length = (lax.axis_size(axis), x.shape[dim])
        up = [(i, (i + 1) % devices) for i in range(devices - 1)]
        down = [(j, i) for i, j in up]
        last = lax.slice_in_dim(x, length - width, length, axis=dim)
        first = lax.slice_in_dim(x, 0, width, axis=dim)
        before = lax.ppermute(last, axis, up)
        after = lax.ppermute(first, axis, down)
        x = jnp.concatenate([before, x, after], axis=dim)
    return x


def views(rimmed):
    return (
        rimmed[..., :-2, 1:-1],
        rimmed[..., 2:, 1:-1],
        rimmed[..., 1:-1, 2:],
        rimmed[..., 1:-1, :-2],
    )


def fold_rows(base, nblocks, pieces):
    values, targets = pieces
    wanted = (base + jnp.arange(nblocks)).astype(jnp.float32)
    onehot = (targets[None, :] == wanted[:, None]).astype(jnp.float32)
    return jnp.dot(onehot, values, precision=highest)


def shards(
    saved_period_abundance,
    final_abundance_sensitivity,
    prey_biomass,
    water_heat_field,
    marine_indicator,
    fishing_pressure,
    offspring_yield,
    death_fraction,
    gear_vulnerability,
    spreading_coefficient,
    directed_drift_rate,
    favoured_thermal_level,
    breeding_contribution,
    landing_error_sensitivity,
    fleet_east_piece,
    fleet_north_piece,
    fleet_area_patch,
    fleet_age_bounds,
):
    months, ages_here, rows_y, rows_x = saved_period_abundance.shape
    coh_pos = lax.axis_index("coh")
    lat_pos = lax.axis_index("lat")
    lon_pos = lax.axis_index("lon")
    lon_count = lax.axis_size("lon")
    total_ages = ages_here * lax.axis_size("coh")
    cohort_age = coh_pos * ages_here + jnp.arange(ages_here)
    maturity = (cohort_age + 1).astype(jnp.float32) / total_ages * breeding_contribution
    sea_field = marine_indicator.astype(jnp.float32)
    row_count = landing_error_sensitivity.shape[0]
    blocks_y = rows_y // BY
    blocks_x = rows_x // BX
    nblocks = blocks_y * blocks_x
    inside = (cohort_age[None, :] >= fleet_age_bounds[:, 0:1]) & (
        cohort_age[None, :] < fleet_age_bounds[:, 1:2]
    )
    masked = (landing_error_sensitivity * inside[:, None, :].astype(jnp.float32)).reshape(
        row_count, months * ages_here
    )
    place_id = (
        (fleet_north_piece * lon_count + fleet_east_piece[:, 0]) * nblocks + fleet_area_patch
    ).astype(jnp.float32)
    block_values = fold_rows(
        (lat_pos * lon_count + lon_pos) * nblocks,
        nblocks,
        (
            lax.all_gather(masked, ("lat", "lon"), axis=0, tiled=True),
            lax.all_gather(place_id, ("lat", "lon"), axis=0, tiled=True),
        ),
    )
    partial_spawn = jnp.stack(
        [
            jnp.tensordot(
                maturity,
                saved_period_abundance[period_counter].astype(jnp.float32),
                axes=1,
                precision=highest,
            )
            for period_counter in range(months)
        ]
    )
    survive = jnp.exp(
        -death_fraction[:, None, None] - gear_vulnerability[:, None, None] * fishing_pressure[None]
    )
    adjoint = final_abundance_sensitivity.astype(jnp.float32)
    grad_recruit = jnp.zeros((rows_y, rows_x), jnp.float32)
    spawn_total = lax.psum(partial_spawn, "coh")
    for period_counter in range(months - 1, -1, -1):
        spawning = spawn_total[period_counter]
        first_plane = from_root(adjoint[0], "coh", 0)
        next_plane = shifted(adjoint[0], "coh", -1)
        extended = jnp.concatenate(
            [
                adjoint[1:],
                next_plane[None],
                prey_biomass[period_counter][None],
                water_heat_field[period_counter][None],
                sea_field[None],
            ],
            axis=0,
        )
        rimmed = with_halo(extended, (("lat", 1), ("lon", 2)), 1)
        later_rim = rimmed[:ages_here]
        forage_rim = rimmed[ages_here]
        thermal_halo_border = rimmed[ages_here + 1]
        sea_rim = rimmed[ages_here + 2]
        thermal_departure = (
            thermal_halo_border[None] - favoured_thermal_level[:, None, None]
        ) / thermal_tolerance_spread
        habitat = sea_rim * forage_rim / (1.0 + thermal_departure * thermal_departure)
        later = later_rim[:, 1:-1, 1:-1]
        habitat_here = habitat[:, 1:-1, 1:-1]
        outflow = jnp.zeros_like(later)
        for sea_next, hab_next, adj_next in zip(views(sea_rim), views(habitat), views(later_rim)):
            flow_rate = (
                sea_field
                * sea_next
                * (
                    spreading_coefficient[:, None, None]
                    + jnp.maximum(
                        directed_drift_rate[:, None, None] * (hab_next - habitat_here), 0.0
                    )
                )
            )
            outflow = outflow + flow_rate * (later - adj_next)
        after_move = later - outflow
        ratio = 1.0 / (1.0 + spawning)
        recruit_term = first_plane * sea_field * offspring_yield * ratio * ratio
        month_values = block_values[
            :, period_counter * ages_here : (period_counter + 1) * ages_here
        ]
        block_grid = month_values.reshape(blocks_y, blocks_x, ages_here).transpose(2, 0, 1)
        spread = jnp.broadcast_to(
            block_grid[:, :, None, :, None], (ages_here, blocks_y, BY, blocks_x, BX)
        )
        adjoint = (
            survive * after_move
            + recruit_term[None] * maturity[:, None, None]
            + gear_vulnerability[:, None, None]
            * fishing_pressure[None]
            * spread.reshape(ages_here, rows_y, rows_x)
        )
        grad_recruit = grad_recruit + first_plane * sea_field * spawning * ratio
    return (adjoint, grad_recruit)


def solution(mesh):
    in_specs = (
        P(None, "coh", "lat", "lon"),
        P("coh", "lat", "lon"),
        P(None, "lat", "lon"),
        P(None, "lat", "lon"),
        P("lat", "lon"),
        P("lat", "lon"),
        P("lat", "lon"),
        P("coh"),
        P("coh"),
        P("coh"),
        P("coh"),
        P("coh"),
        P("coh"),
        P(("lat", "lon"), None, "coh"),
        P(("lat", "lon"), None),
        P(("lat", "lon")),
        P(("lat", "lon")),
        P(("lat", "lon"), None),
    )
    out_specs = (P("coh", "lat", "lon"), P("lat", "lon"))
    return jax.shard_map(shards, mesh=mesh, in_specs=in_specs, out_specs=out_specs, check_vma=False)
```

profile of v0, /device:TPU:2, one launch (start us, length us, event | category | flops | bytes accessed | tf_op | source)
XLA Modules:
  0.0 357.3 jit_solution(8194302968326700372)
XLA Ops:
  15.1 1.8 constant_dynamic-update-slice_fusion.1
  17.1 53.0 %all_gather.7 = f32[2048,64]{1,0:T(8,128)S(1)} all-gather(f32[32,64]{1,0:T(8,128)S(1)} %reshape.100), channel_id=1, replica_groups=mesh['coh'=4,'lat'=4,'lon'=16] {'lat','lon'}, dimensions={0}, use_global_device_ids=true | all-gather | bytes 532480 | tf_op jit(solution)/shard_map/all_gather | solution.py:98
  72.9 109.3 %all-reduce = f32[2048]{0:T(1024)S(1)} all-reduce(f32[2048]{0:T(1024)S(1)} %convert_dynamic-update-slice_fusion), channel_id=1, replica_groups=mesh['coh'=4,'lat'=4,'lon'=16] {'lat','lon'}, use_global_device_ids=true, to_apply=%add | all-reduce | flops 2048 | bytes 16384
  184.1 22.3 %collective-permute-start.2 = (f32[35,1,256]{2,1,0:T(1,128)S(1)}, f32[35,1,256]{2,1,0:T(1,128)S(1)}, u32[]{:S(2)}, u32[]{:S(2)}) collective-permute-start(f32[35,1,256]{2,1,0:T(1,128)S(1)} %get-tuple-element.17), channel_id=1, source_target_pairs={{16,0},{32,16},{48,32},{17,1},{33,17},{49,33},{18,2},{34,18},{50,3... | collective-permute-start | bytes 107528 | tf_op jit(solution)/shard_map/ppermute | solution.py:31
  206.4 1.9 collective-permute-start.1
  208.8 3.4 collective-permute-done.1
  212.6 1.9 fusion.82
  214.5 1.9 copy.35
  217.6 1.8 copy.36
  222.7 3.9 %broadcast_in_dim.18 = f32[32,4,16,8,32]{4,3,2,1,0:T(8,128)} broadcast(f32[32,4,8]{2,1,0:T(4,128)S(1)} %copy.41), dimensions={0,1,3} | broadcast | bytes 2101248 | tf_op jit(solution)/shard_map/broadcast_in_dim | solution.py:164
  226.6 7.0 %reshape.102 = f32[32,64,256]{2,1,0:T(8,128)} reshape(f32[32,4,16,8,32]{4,3,2,1,0:T(8,128)} %broadcast_in_dim.18) | data formatting | bytes 4194304 | tf_op jit(solution)/shard_map/reshape | solution.py:172
  242.0 13.6 %fusion.4 = f32[32,64,256]{2,1,0:T(8,128)S(1)} fusion(f32[32,64,256]{2,1,0:T(8,128)} %reshape.102, f32[35,66,1]{2,1,0:T(8,128)} %copy.37, f32[35,1,256]{2,1,0:T(1,128)} %copy-done.12, f32[35,64,256]{2,1,0:T(8,128)} %copy-done, f32[35,1,256]{2,1,0:T(1,128)} %copy-done.14, f32[32,66,258]{2,1,0:T(8,128)S(1)} %add_divide_fusion.1, f32[35,66,1]{2,1,0:T(8,128)} %copy.38, ...), kind=kLoop, calls=%fused_computation.11 | loop fusion | flops 25165824 | bytes 19554992 | tf_op jit(solution)/shard_map/add | solution.py:168
  257.0 1.8 fusion.85
  258.8 4.0 %collective-permute-done.5 = f32[64,256]{1,0:T(8,128)S(1)} collective-permute-done((f32[64,256]{1,0:T(8,128)S(1)}, f32[64,256]{1,0:T(8,128)S(1)}, u32[]{:S(2)}, u32[]{:S(2)}) %collective-permute-start.5) | collective-permute-done | bytes 65568 | tf_op jit(solution)/shard_map/ppermute | solution.py:20
  262.9 1.9 collective-permute-start.7
  264.8 3.9 %collective-permute-start.6 = (f32[35,1,256]{2,1,0:T(1,128)S(1)}, f32[35,1,256]{2,1,0:T(1,128)S(1)}, u32[]{:S(2)}, u32[]{:S(2)}) collective-permute-start(f32[35,1,256]{2,1,0:T(1,128)S(1)} %get-tuple-element.14), channel_id=1, source_target_pairs={{0,16},{16,32},{32,48},{1,17},{17,33},{33,49},{2,18},{18,34},{34,5... | collective-permute-start | bytes 107528 | tf_op jit(solution)/shard_map/ppermute | solution.py:30
  268.9 3.9 %broadcast_in_dim.20 = f32[32,4,16,8,32]{4,3,2,1,0:T(8,128)} broadcast(f32[32,4,8]{2,1,0:T(4,128)S(1)} %copy.48), dimensions={0,1,3} | broadcast | bytes 2101248 | tf_op jit(solution)/shard_map/broadcast_in_dim | solution.py:164
  272.8 7.0 %reshape.104 = f32[32,64,256]{2,1,0:T(8,128)} reshape(f32[32,4,16,8,32]{4,3,2,1,0:T(8,128)} %broadcast_in_dim.20) | data formatting | bytes 4194304 | tf_op jit(solution)/shard_map/reshape | solution.py:172
  280.2 1.9 fusion.81
  282.1 1.8 copy.42
  285.4 1.8 copy.43
  296.8 37.3 %all-reduce.5.cloned.1.call-done = f32[64,256]{1,0:T(8,128)} async-done(((f32[64,256]{1,0:T(8,128)}), f32[64,256]{1,0:T(8,128)}) %all-reduce.5.cloned.1.call-update) | async-done | bytes 65552 | tf_op jit(solution)/shard_map/psum | solution.py:14
  334.1 1.9 multiply_add_fusion
  336.1 14.3 %fusion.6 = f32[32,64,256]{2,1,0:T(8,128)} fusion(f32[32,64,256]{2,1,0:T(8,128)} %reshape.104, f32[35,66,1]{2,1,0:T(8,128)} %copy.44, f32[35,1,256]{2,1,0:T(1,128)} %copy-done.11, f32[35,64,256]{2,1,0:T(8,128)} %copy-done.1, f32[35,1,256]{2,1,0:T(1,128)} %copy-done.13, f32[32,66,258]{2,1,0:T(8,128)S(1)} %add_divide_fusion, f32[35,66,1]{2,1,0:T(8,128)} %copy.45, ...), kind=kLoop, calls=%fused_computation.13 | loop fusion | flops 25165824 | bytes 19554992 | tf_op jit(solution)/shard_map/add | solution.py:168
  (129 shorter events, 38.6 us)
Async XLA Ops:
  7.2 233.5 %all-reduce.7.cloned.1.call-start = ((), (), s32[]{:S(2)}) async-start(), calls=%async_computation.1 | async-start | bytes 393216 | tf_op jit(solution)/shard_map/psum | solution.py:14
  8.7 173.6 %collective-permute-start = (f32[64,256]{1,0:T(8,128)S(1)}, f32[64,256]{1,0:T(8,128)S(1)}, u32[]{:S(2)}, u32[]{:S(2)}) collective-permute-start(f32[64,256]{1,0:T(8,128)S(1)} %slice_bitcast_fusion.5), channel_id=1, source_target_pairs={{64,0},{128,64},{192,128},{65,1},{129,65},{193,129},{66,2},{130,66... | collective-permute-start | bytes 196616 | tf_op jit(solution)/shard_map/ppermute | solution.py:20
  15.0 319.1 %all-reduce.5.cloned.1.call-start = ((), (), s32[]{:S(2)}) async-start(), calls=%async_computation | async-start | bytes 131072 | tf_op jit(solution)/shard_map/psum | solution.py:14
  15.1 168.9 %copy-start.9 = (s32[64,256]{1,0:T(8,128)S(1)}, s32[64,256]{1,0:T(8,128)}, u32[]{:S(2)}) copy-start(s32[64,256]{1,0:T(8,128)} %param.22) | copy-start | bytes 196612
  182.3 24.1 %copy-start.15 = (f32[64,256]{1,0:T(8,128)}, f32[64,256]{1,0:T(8,128)S(1)}, u32[]{:S(2)}) copy-start(f32[64,256]{1,0:T(8,128)S(1)} %collective-permute-done) | copy-start | bytes 196612
  184.0 54.4 %copy-start = (f32[35,64,256]{2,1,0:T(8,128)}, f32[35,64,256]{2,1,0:T(8,128)S(1)}, u32[]{:S(2)}) copy-start(f32[35,64,256]{2,1,0:T(8,128)S(1)} %bitcast_dynamic-update-slice_fusion.1) | copy-start | bytes 6881284
  184.1 24.7 %collective-permute-start.2 = (f32[35,1,256]{2,1,0:T(1,128)S(1)}, f32[35,1,256]{2,1,0:T(1,128)S(1)}, u32[]{:S(2)}, u32[]{:S(2)}) collective-permute-start(f32[35,1,256]{2,1,0:T(1,128)S(1)} %get-tuple-element.17), channel_id=1, source_target_pairs={{16,0},{32,16},{48,32},{17,1},{33,17},{49,33},{18,2},{34,18},{50,3... | collective-permute-start | bytes 107528 | tf_op jit(solution)/shard_map/ppermute | solution.py:31
  206.4 5.8 %collective-permute-start.1 = (f32[35,1,256]{2,1,0:T(1,128)S(1)}, f32[35,1,256]{2,1,0:T(1,128)S(1)}, u32[]{:S(2)}, u32[]{:S(2)}) collective-permute-start(f32[35,1,256]{2,1,0:T(1,128)S(1)} %get-tuple-element.16), channel_id=1, source_target_pairs={{0,16},{16,32},{32,48},{1,17},{17,33},{33,49},{2,18},{18,34},{34,5... | collective-permute-start | bytes 107528 | tf_op jit(solution)/shard_map/ppermute | solution.py:30
  208.8 29.6 %copy-start.12 = (f32[35,1,256]{2,1,0:T(1,128)}, f32[35,1,256]{2,1,0:T(1,128)S(1)}, u32[]{:S(2)}) copy-start(f32[35,1,256]{2,1,0:T(1,128)S(1)} %collective-permute-done.2) | copy-start | bytes 107524
  212.2 26.2 %copy-start.14 = (f32[35,1,256]{2,1,0:T(1,128)}, f32[35,1,256]{2,1,0:T(1,128)S(1)}, u32[]{:S(2)}) copy-start(f32[35,1,256]{2,1,0:T(1,128)S(1)} %collective-permute-done.1) | copy-start | bytes 107524
  216.3 17.9 %collective-permute-start.3 = (f32[35,66,1]{1,2,0:T(1,128)S(1)}, f32[35,66,1]{1,2,0:T(1,128)S(1)}, u32[]{:S(2)}, u32[]{:S(2)}) collective-permute-start(f32[35,66,1]{1,2,0:T(1,128)S(1)} %copy.35), channel_id=1, source_target_pairs={{0,1},{1,2},{2,3},{3,4},{4,5},{5,6},{6,7},{7,8},{8,9},{9,10},{10,1... | collective-permute-start | bytes 27728 | tf_op jit(solution)/shard_map/ppermute | solution.py:30
  219.4 16.4 %collective-permute-start.4 = (f32[35,66,1]{1,2,0:T(1,128)S(1)}, f32[35,66,1]{1,2,0:T(1,128)S(1)}, u32[]{:S(2)}, u32[]{:S(2)}) collective-permute-start(f32[35,66,1]{1,2,0:T(1,128)S(1)} %copy.36), channel_id=1, source_target_pairs={{1,0},{2,1},{3,2},{4,3},{5,4},{6,5},{7,6},{8,7},{9,8},{10,9},{11,1... | collective-permute-start | bytes 27728 | tf_op jit(solution)/shard_map/ppermute | solution.py:31
  255.6 7.2 %collective-permute-start.5 = (f32[64,256]{1,0:T(8,128)S(1)}, f32[64,256]{1,0:T(8,128)S(1)}, u32[]{:S(2)}, u32[]{:S(2)}) collective-permute-start(f32[64,256]{1,0:T(8,128)S(1)} %slice_bitcast_fusion.3), channel_id=1, source_target_pairs={{64,0},{128,64},{192,128},{65,1},{129,65},{193,129},{66,2},{130,66... | collective-permute-start | bytes 196616 | tf_op jit(solution)/shard_map/ppermute | solution.py:20
  262.8 31.7 %copy-start.1 = (f32[35,64,256]{2,1,0:T(8,128)}, f32[35,64,256]{2,1,0:T(8,128)S(1)}, u32[]{:S(2)}) copy-start(f32[35,64,256]{2,1,0:T(8,128)S(1)} %bitcast_dynamic-update-slice_fusion) | copy-start | bytes 6881284
  262.9 16.9 %collective-permute-start.7 = (f32[35,1,256]{2,1,0:T(1,128)S(1)}, f32[35,1,256]{2,1,0:T(1,128)S(1)}, u32[]{:S(2)}, u32[]{:S(2)}) collective-permute-start(f32[35,1,256]{2,1,0:T(1,128)S(1)} %get-tuple-element.15), channel_id=1, source_target_pairs={{16,0},{32,16},{48,32},{17,1},{33,17},{49,33},{18,2},{34,18},{50,3... | collective-permute-start | bytes 107528 | tf_op jit(solution)/shard_map/ppermute | solution.py:31
  264.8 15.0 %collective-permute-start.6 = (f32[35,1,256]{2,1,0:T(1,128)S(1)}, f32[35,1,256]{2,1,0:T(1,128)S(1)}, u32[]{:S(2)}, u32[]{:S(2)}) collective-permute-start(f32[35,1,256]{2,1,0:T(1,128)S(1)} %get-tuple-element.14), channel_id=1, source_target_pairs={{0,16},{16,32},{32,48},{1,17},{17,33},{33,49},{2,18},{18,34},{34,5... | collective-permute-start | bytes 107528 | tf_op jit(solution)/shard_map/ppermute | solution.py:30
  279.8 14.7 %copy-start.11 = (f32[35,1,256]{2,1,0:T(1,128)}, f32[35,1,256]{2,1,0:T(1,128)S(1)}, u32[]{:S(2)}) copy-start(f32[35,1,256]{2,1,0:T(1,128)S(1)} %collective-permute-done.7) | copy-start | bytes 107524
  279.8 14.7 %copy-start.13 = (f32[35,1,256]{2,1,0:T(1,128)}, f32[35,1,256]{2,1,0:T(1,128)S(1)}, u32[]{:S(2)}) copy-start(f32[35,1,256]{2,1,0:T(1,128)S(1)} %collective-permute-done.6) | copy-start | bytes 107524
  283.8 6.4 %collective-permute-start.8 = (f32[35,66,1]{1,2,0:T(1,128)S(1)}, f32[35,66,1]{1,2,0:T(1,128)S(1)}, u32[]{:S(2)}, u32[]{:S(2)}) collective-permute-start(f32[35,66,1]{1,2,0:T(1,128)S(1)} %copy.42), channel_id=1, source_target_pairs={{0,1},{1,2},{2,3},{3,4},{4,5},{5,6},{6,7},{7,8},{8,9},{9,10},{10,1... | collective-permute-start | bytes 27728 | tf_op jit(solution)/shard_map/ppermute | solution.py:30
  287.2 4.6 %collective-permute-start.9 = (f32[35,66,1]{1,2,0:T(1,128)S(1)}, f32[35,66,1]{1,2,0:T(1,128)S(1)}, u32[]{:S(2)}, u32[]{:S(2)}) collective-permute-start(f32[35,66,1]{1,2,0:T(1,128)S(1)} %copy.43), channel_id=1, source_target_pairs={{1,0},{2,1},{3,2},{4,3},{5,4},{6,5},{7,6},{8,7},{9,8},{10,9},{11,1... | collective-permute-start | bytes 27728 | tf_op jit(solution)/shard_map/ppermute | solution.py:31
  296.0 40.0 %copy-start.21 = (f32[32]{0:T(128)S(1)}, f32[32]{0:T(128)}, u32[]{:S(2)}) copy-start(f32[32]{0:T(128)} %copy-done.20) | copy-start | bytes 388
  296.0 40.0 %copy-start.22 = (f32[32]{0:T(128)S(1)}, f32[32]{0:T(128)}, u32[]{:S(2)}) copy-start(f32[32]{0:T(128)} %param.28) | copy-start | bytes 388
  296.0 40.0 %copy-start.23 = (f32[32]{0:T(128)S(1)}, f32[32]{0:T(128)}, u32[]{:S(2)}) copy-start(f32[32]{0:T(128)} %param.27) | copy-start | bytes 388
  296.0 40.0 %copy-start.24 = (f32[32]{0:T(128)S(1)}, f32[32]{0:T(128)}, u32[]{:S(2)}) copy-start(f32[32]{0:T(128)} %param.26) | copy-start | bytes 388
  (18 other events, 66.1 us)
Sparse Core Ops, SparseCore 0:
  15.2 50.9 all-reduce.6
  290.4 43.6 all-reduce.4
where the time goes:
time: 358 us; the launch traced here: 357 us
  blocking collectives  162 us (45%)
  local copies, waits for them, and re-layouts  51 us (14%)
  waiting for transfers between devices  44.8 us (13%)
  other arithmetic  42.6 us (12%)
  starting transfers between devices  38.8 us (11%)
  between operations  15.3 us (4%)
    unnamed x1, blocking collectives  109 us
    all_gather x1, blocking collectives, shards(): lax.all_gather(masked, ('lat', 'lon'), axis=0, tiled=True)  53 us
    psum x2, waiting for transfers between devices, from_root(): return lax.psum(kept, axis)  37.3 us
    add x2, other arithmetic, shards(): survive * after_move + recruit_term[None] * maturity[:, None, None]  27.9 us
    ppermute x4, starting transfers between devices, with_halo(): after = lax.ppermute(first, axis, down)  27.2 us
    reshape x2, local copies, waits for them, and re-layouts, shards(): spread.reshape(ages_here, rows_y, rows_x)  14.1 us
    ppermute x4, starting transfers between devices, with_halo(): before = lax.ppermute(last, axis, up)  8.77 us
    broadcast_in_dim x2, local copies, waits for them, and re-layouts, shards(): jnp.broadcast_to(block_grid[:, :, None, :, None], (ages_here, blocks_y, B...  7.82 us
  transfers between devices with their start and end apart: 12, of which 3 were waited for; matrix products, arithmetic and copies ran while one was open for 16% of the time, Pallas kernels for 0%

commit v1 on v0

--- a/solution.py
+++ b/solution.py
@@ -9,9 +9,15 @@
 highest = lax.Precision.HIGHEST
 
 
+def gather_and_add(x, axis):
+    parts = lax.all_gather(x, axis, axis=0, tiled=False)
+    acc = parts.sum(axis=0)
+    return acc
+
+
 def from_root(value, axis, source):
     kept = jnp.where(lax.axis_index(axis) == source, value, 0).astype(value.dtype)
-    return lax.psum(kept, axis)
+    return gather_and_add(kept, axis)
 
 
 def shifted(block, axis, distance):

time: 358 us -> 342 us (0.955)
  waiting for transfers between devices: 44.8 us -> 6.94 us
  blocking collectives: 162 us -> 190 us
  other arithmetic: 42.6 us -> 34.6 us
    psum x2 -> x1, waiting for transfers between devices: 37.3 us -> 0.02 us  [shards(): spawn_total = lax.psum(partial_spawn, 'coh')]
    all_gather x0 -> x2, blocking collectives: none -> 27.6 us  [gather_and_add(): parts = lax.all_gather(x, axis, axis=0, tiled=False)]
    add x2, other arithmetic: 27.9 us -> 22.5 us  [shards(): survive * after_move + recruit_term[None] * maturity[:, None, None]]
    unnamed x69 -> x75, local copies, waits for them, and re-layouts: 6.18 us -> 7.35 us
  transfers between devices with their start and end apart: 12 -> 11, of which waited for: 3 -> 2; matrix products, arithmetic and copies ran while one was open for 16% -> 16% of each run, Pallas kernels for 0% -> 0%
where the time goes in v1:
time: 342 us; the launch traced here: 341 us
  blocking collectives  190 us (56%)
  local copies, waits for them, and re-layouts  53.5 us (16%)
  starting transfers between devices  38 us (11%)
  other arithmetic  34.6 us (10%)
  between operations  15.3 us (4%)
  waiting for transfers between devices  6.94 us (2%)
    unnamed x1, blocking collectives  109 us
    all_gather x1, blocking collectives, shards(): lax.all_gather(masked, ('lat', 'lon'), axis=0, tiled=True)  53 us
    all_gather x2, blocking collectives, gather_and_add(): parts = lax.all_gather(x, axis, axis=0, tiled=False)  27.6 us
    ppermute x4, starting transfers between devices, with_halo(): after = lax.ppermute(first, axis, down)  26.8 us
    add x2, other arithmetic, shards(): survive * after_move + recruit_term[None] * maturity[:, None, None]  22.5 us
    reshape x2, local copies, waits for them, and re-layouts, shards(): spread.reshape(ages_here, rows_y, rows_x)  14.1 us
    ppermute x4, starting transfers between devices, with_halo(): before = lax.ppermute(last, axis, up)  8.46 us
    slice x4, local copies, waits for them, and re-layouts, with_halo(): first = lax.slice_in_dim(x, 0, width, axis=dim)  7.96 us
  transfers between devices with their start and end apart: 11, of which 2 were waited for; matrix products, arithmetic and copies ran while one was open for 16% of the time, Pallas kernels for 0%

profile of v1, /device:TPU:2, one launch (start us, length us, event | category | flops | bytes accessed | tf_op | source)
XLA Modules:
  0.0 340.8 jit_solution(8174303705523858963)
XLA Ops:
  17.1 53.0 %all_gather.16 = f32[2048,64]{1,0:T(8,128)S(1)} all-gather(f32[32,64]{1,0:T(8,128)S(1)} %reshape.100), channel_id=1, replica_groups=mesh['coh'=4,'lat'=4,'lon'=16] {'lat','lon'}, dimensions={0}, use_global_device_ids=true | all-gather | bytes 532480 | tf_op jit(solution)/shard_map/all_gather | solution.py:104
  72.9 109.3 %all-reduce = f32[2048]{0:T(1024)S(1)} all-reduce(f32[2048]{0:T(1024)S(1)} %convert_dynamic-update-slice_fusion), channel_id=1, replica_groups=mesh['coh'=4,'lat'=4,'lon'=16] {'lat','lon'}, use_global_device_ids=true, to_apply=%add | all-reduce | flops 2048 | bytes 16384
  184.6 22.3 %collective-permute-start.2 = (f32[35,1,256]{2,1,0:T(1,128)S(1)}, f32[35,1,256]{2,1,0:T(1,128)S(1)}, u32[]{:S(2)}, u32[]{:S(2)}) collective-permute-start(f32[35,1,256]{2,1,0:T(1,128)S(1)} %get-tuple-element.15), channel_id=1, source_target_pairs={{16,0},{32,16},{48,32},{17,1},{33,17},{49,33},{18,2},{34,18},{50,3... | collective-permute-start | bytes 107528 | tf_op jit(solution)/shard_map/ppermute | solution.py:37
  206.9 1.9 collective-permute-start.1
  208.9 3.8 %collective-permute-done.1 = f32[35,1,256]{2,1,0:T(1,128)S(1)} collective-permute-done((f32[35,1,256]{2,1,0:T(1,128)S(1)}, f32[35,1,256]{2,1,0:T(1,128)S(1)}, u32[]{:S(2)}, u32[]{:S(2)}) %collective-permute-start.1) | collective-permute-done | bytes 35872 | tf_op jit(solution)/shard_map/ppermute | solution.py:36
  213.0 1.9 fusion.82
  215.0 1.9 copy.37
  218.1 2.4 copy.38
  221.8 15.0 %all_gather.14 = f32[4,64,256]{2,1,0:T(8,128)} all-gather(f32[1,64,256]{2,1,0:T(8,128)S(1)} %get-tuple-element.22), channel_id=1, replica_groups=mesh['coh'=4,'lat'=4,'lon'=16] {'coh'}, dimensions={0}, use_global_device_ids=true | all-gather | bytes 327680 | tf_op jit(solution)/shard_map/all_gather | solution.py:13
  238.5 3.9 %broadcast_in_dim.18 = f32[32,4,16,8,32]{4,3,2,1,0:T(8,128)} broadcast(f32[32,4,8]{2,1,0:T(4,128)S(1)} %copy.43), dimensions={0,1,3} | broadcast | bytes 2101248 | tf_op jit(solution)/shard_map/broadcast_in_dim | solution.py:170
  242.4 7.1 %reshape.102 = f32[32,64,256]{2,1,0:T(8,128)} reshape(f32[32,4,16,8,32]{4,3,2,1,0:T(8,128)} %broadcast_in_dim.18) | data formatting | bytes 4194304 | tf_op jit(solution)/shard_map/reshape | solution.py:178
  252.2 2.3 copy.40
  259.1 13.5 %fusion.4 = f32[32,64,256]{2,1,0:T(8,128)S(1)} fusion(f32[32,64,256]{2,1,0:T(8,128)} %reshape.102, f32[35,66,1]{2,1,0:T(8,128)} %copy.39, f32[35,1,256]{2,1,0:T(1,128)} %copy-done.13, f32[35,64,256]{2,1,0:T(8,128)} %copy-done, f32[35,1,256]{2,1,0:T(1,128)} %copy-done.14, f32[32,66,258]{2,1,0:T(8,128)S(1)} %add_divide_fusion.1, f32[35,66,1]{2,1,0:T(8,128)} %copy.40, ...), kind=kLoop, calls=%fused_computation.11 | loop fusion | flops 25165824 | bytes 19554992 | tf_op jit(solution)/shard_map/add | solution.py:174
  274.1 1.8 fusion.85
  275.9 3.0 collective-permute-done.5
  279.1 1.9 collective-permute-start.7
  281.1 3.9 %collective-permute-start.6 = (f32[35,1,256]{2,1,0:T(1,128)S(1)}, f32[35,1,256]{2,1,0:T(1,128)S(1)}, u32[]{:S(2)}, u32[]{:S(2)}) collective-permute-start(f32[35,1,256]{2,1,0:T(1,128)S(1)} %get-tuple-element.12), channel_id=1, source_target_pairs={{0,16},{16,32},{32,48},{1,17},{17,33},{33,49},{2,18},{18,34},{34,5... | collective-permute-start | bytes 107528 | tf_op jit(solution)/shard_map/ppermute | solution.py:36
  285.1 3.9 %broadcast_in_dim.20 = f32[32,4,16,8,32]{4,3,2,1,0:T(8,128)} broadcast(f32[32,4,8]{2,1,0:T(4,128)S(1)} %copy.50), dimensions={0,1,3} | broadcast | bytes 2101248 | tf_op jit(solution)/shard_map/broadcast_in_dim | solution.py:170
  289.0 7.0 %reshape.104 = f32[32,64,256]{2,1,0:T(8,128)} reshape(f32[32,4,16,8,32]{4,3,2,1,0:T(8,128)} %broadcast_in_dim.20) | data formatting | bytes 4194304 | tf_op jit(solution)/shard_map/reshape | solution.py:178
  296.4 1.9 fusion.81
  298.2 1.8 copy.44
  301.3 1.8 copy.45
  304.4 12.7 %all_gather.17 = f32[4,64,256]{2,1,0:T(8,128)S(1)} all-gather(f32[1,64,256]{2,1,0:T(8,128)S(1)} %get-tuple-element.16), channel_id=1, replica_groups=mesh['coh'=4,'lat'=4,'lon'=16] {'coh'}, dimensions={0}, use_global_device_ids=true | all-gather | bytes 327680 | tf_op jit(solution)/shard_map/all_gather | solution.py:13
  325.0 9.0 %fusion.6 = f32[32,64,256]{2,1,0:T(8,128)} fusion(f32[32,64,256]{2,1,0:T(8,128)S(1)} %copy-done.6, f32[35,66,1]{2,1,0:T(8,128)S(1)} %copy-done.1, f32[35,1,256]{2,1,0:T(1,128)S(1)} %collective-permute-done.7, f32[35,64,256]{2,1,0:T(8,128)S(1)} %bitcast_dynamic-update-slice_fusion, f32[35,1,256]{2,1,0:T(1,128)S(1)} %collective-permute-done.6, ...), kind=kLoop, calls=%fused_computation.13 | loop fusion | flops 25165824 | bytes 19554992 | tf_op jit(solution)/shard_map/add | solution.py:174
  (134 shorter events, 38.5 us)
Async XLA Ops:
  7.2 250.7 %all-reduce.3.cloned.1.call-start = ((), (), s32[]{:S(2)}) async-start(), calls=%async_computation | async-start | bytes 262144 | tf_op jit(solution)/shard_map/psum | solution.py:124
  8.7 3.7 %copy-start.7 = (f32[32,64,256]{2,1,0:T(8,128)}, f32[32,64,256]{2,1,0:T(8,128)S(1)}, u32[]{:S(2)}) copy-start(f32[32,64,256]{2,1,0:T(8,128)S(1)} %convert_element_type.33) | copy-start | bytes 6291460
  9.4 173.3 %collective-permute-start = (f32[64,256]{1,0:T(8,128)}, f32[64,256]{1,0:T(8,128)S(1)}, u32[]{:S(2)}, u32[]{:S(2)}) collective-permute-start(f32[64,256]{1,0:T(8,128)} %get-tuple-element.23), channel_id=1, source_target_pairs={{64,0},{128,64},{192,128},{65,1},{129,65},{193,129},{66,2},{130,66... | collective-permute-start | bytes 196616 | tf_op jit(solution)/shard_map/ppermute | solution.py:26
  12.4 2.7 copy-start.22
  16.9 167.6 %copy-start.10 = (s32[64,256]{1,0:T(8,128)S(1)}, s32[64,256]{1,0:T(8,128)}, u32[]{:S(2)}) copy-start(s32[64,256]{1,0:T(8,128)} %param.22) | copy-start | bytes 196612
  182.8 24.1 %copy-start.17 = (f32[64,256]{1,0:T(8,128)}, f32[64,256]{1,0:T(8,128)S(1)}, u32[]{:S(2)}) copy-start(f32[64,256]{1,0:T(8,128)S(1)} %collective-permute-done) | copy-start | bytes 196612
  184.5 71.1 %copy-start = (f32[35,64,256]{2,1,0:T(8,128)}, f32[35,64,256]{2,1,0:T(8,128)S(1)}, u32[]{:S(2)}) copy-start(f32[35,64,256]{2,1,0:T(8,128)S(1)} %bitcast_dynamic-update-slice_fusion.1) | copy-start | bytes 6881284
  184.6 24.3 %collective-permute-start.2 = (f32[35,1,256]{2,1,0:T(1,128)S(1)}, f32[35,1,256]{2,1,0:T(1,128)S(1)}, u32[]{:S(2)}, u32[]{:S(2)}) collective-permute-start(f32[35,1,256]{2,1,0:T(1,128)S(1)} %get-tuple-element.15), channel_id=1, source_target_pairs={{16,0},{32,16},{48,32},{17,1},{33,17},{49,33},{18,2},{34,18},{50,3... | collective-permute-start | bytes 107528 | tf_op jit(solution)/shard_map/ppermute | solution.py:37
  206.9 5.8 %collective-permute-start.1 = (f32[35,1,256]{2,1,0:T(1,128)S(1)}, f32[35,1,256]{2,1,0:T(1,128)S(1)}, u32[]{:S(2)}, u32[]{:S(2)}) collective-permute-start(f32[35,1,256]{2,1,0:T(1,128)S(1)} %get-tuple-element.14), channel_id=1, source_target_pairs={{0,16},{16,32},{32,48},{1,17},{17,33},{33,49},{2,18},{18,34},{34,5... | collective-permute-start | bytes 107528 | tf_op jit(solution)/shard_map/ppermute | solution.py:36
  208.9 46.7 %copy-start.13 = (f32[35,1,256]{2,1,0:T(1,128)}, f32[35,1,256]{2,1,0:T(1,128)S(1)}, u32[]{:S(2)}) copy-start(f32[35,1,256]{2,1,0:T(1,128)S(1)} %collective-permute-done.2) | copy-start | bytes 107524
  212.7 42.9 %copy-start.14 = (f32[35,1,256]{2,1,0:T(1,128)}, f32[35,1,256]{2,1,0:T(1,128)S(1)}, u32[]{:S(2)}) copy-start(f32[35,1,256]{2,1,0:T(1,128)S(1)} %collective-permute-done.1) | copy-start | bytes 107524
  215.0 21.8 %copy-start.5 = (bf16[32,64,256]{2,1,0:T(8,128)(2,1)S(1)}, bf16[32,64,256]{2,1,0:T(8,128)(2,1)}, u32[]{:S(2)}) copy-start(bf16[32,64,256]{2,1,0:T(8,128)(2,1)} %param.19) | copy-start | bytes 3145732
  216.8 33.8 %collective-permute-start.3 = (f32[35,66,1]{1,2,0:T(1,128)S(1)}, f32[35,66,1]{1,2,0:T(1,128)S(1)}, u32[]{:S(2)}, u32[]{:S(2)}) collective-permute-start(f32[35,66,1]{1,2,0:T(1,128)S(1)} %copy.37), channel_id=1, source_target_pairs={{0,1},{1,2},{2,3},{3,4},{4,5},{5,6},{6,7},{7,8},{8,9},{9,10},{10,1... | collective-permute-start | bytes 27728 | tf_op jit(solution)/shard_map/ppermute | solution.py:36
  220.5 31.7 %collective-permute-start.4 = (f32[35,66,1]{1,2,0:T(1,128)}, f32[35,66,1]{1,2,0:T(1,128)}, u32[]{:S(2)}, u32[]{:S(2)}) collective-permute-start(f32[35,66,1]{1,2,0:T(1,128)} %copy.38), channel_id=1, source_target_pairs={{1,0},{2,1},{3,2},{4,3},{5,4},{6,5},{7,6},{8,7},{9,8},{10,9},{11,1... | collective-permute-start | bytes 27728 | tf_op jit(solution)/shard_map/ppermute | solution.py:37
  242.4 7.1 %copy-start.9 = (f32[4,64,256]{2,1,0:T(8,128)S(1)}, f32[4,64,256]{2,1,0:T(8,128)}, u32[]{:S(2)}) copy-start(f32[4,64,256]{2,1,0:T(8,128)} %all_gather.14) | copy-start | bytes 786436
  242.4 7.7 %copy-start.32 = (f32[32]{0:T(128)S(1)}, f32[32]{0:T(128)}, u32[]{:S(2)}) copy-start(f32[32]{0:T(128)} %param.25) | copy-start | bytes 388
  272.7 6.3 %copy-start.19 = (f32[2,64,256]{2,1,0:T(8,128)S(1)}, f32[2,64,256]{2,1,0:T(8,128)}, u32[]{:S(2)}) copy-start(f32[2,64,256]{2,1,0:T(8,128)} %param.20) | copy-start | bytes 393220
  272.7 6.3 %copy-start.20 = (f32[2,64,256]{2,1,0:T(8,128)S(1)}, f32[2,64,256]{2,1,0:T(8,128)}, u32[]{:S(2)}) copy-start(f32[2,64,256]{2,1,0:T(8,128)} %param.21) | copy-start | bytes 393220
  272.7 6.4 %copy-start.11 = (s32[64,256]{1,0:T(8,128)S(1)}, s32[64,256]{1,0:T(8,128)}, u32[]{:S(2)}) copy-start(s32[64,256]{1,0:T(8,128)} %param.22) | copy-start | bytes 196612
  272.7 6.3 %collective-permute-start.5 = (f32[64,256]{1,0:T(8,128)S(1)}, f32[64,256]{1,0:T(8,128)S(1)}, u32[]{:S(2)}, u32[]{:S(2)}) collective-permute-start(f32[64,256]{1,0:T(8,128)S(1)} %get-tuple-element.17), channel_id=1, source_target_pairs={{64,0},{128,64},{192,128},{65,1},{129,65},{193,129},{66,2},{130,66... | collective-permute-start | bytes 196616 | tf_op jit(solution)/shard_map/ppermute | solution.py:26
  279.1 16.9 %collective-permute-start.7 = (f32[35,1,256]{2,1,0:T(1,128)S(1)}, f32[35,1,256]{2,1,0:T(1,128)S(1)}, u32[]{:S(2)}, u32[]{:S(2)}) collective-permute-start(f32[35,1,256]{2,1,0:T(1,128)S(1)} %get-tuple-element.13), channel_id=1, source_target_pairs={{16,0},{32,16},{48,32},{17,1},{33,17},{49,33},{18,2},{34,18},{50,3... | collective-permute-start | bytes 107528 | tf_op jit(solution)/shard_map/ppermute | solution.py:37
  281.1 15.0 %collective-permute-start.6 = (f32[35,1,256]{2,1,0:T(1,128)S(1)}, f32[35,1,256]{2,1,0:T(1,128)S(1)}, u32[]{:S(2)}, u32[]{:S(2)}) collective-permute-start(f32[35,1,256]{2,1,0:T(1,128)S(1)} %get-tuple-element.12), channel_id=1, source_target_pairs={{0,16},{16,32},{32,48},{1,17},{17,33},{33,49},{2,18},{18,34},{34,5... | collective-permute-start | bytes 107528 | tf_op jit(solution)/shard_map/ppermute | solution.py:36
  300.0 17.1 %collective-permute-start.8 = (f32[35,66,1]{1,2,0:T(1,128)S(1)}, f32[35,66,1]{1,2,0:T(1,128)S(1)}, u32[]{:S(2)}, u32[]{:S(2)}) collective-permute-start(f32[35,66,1]{1,2,0:T(1,128)S(1)} %copy.44), channel_id=1, source_target_pairs={{0,1},{1,2},{2,3},{3,4},{4,5},{5,6},{6,7},{7,8},{8,9},{9,10},{10,1... | collective-permute-start | bytes 27728 | tf_op jit(solution)/shard_map/ppermute | solution.py:36
  303.1 15.6 %collective-permute-start.9 = (f32[35,66,1]{1,2,0:T(1,128)S(1)}, f32[35,66,1]{1,2,0:T(1,128)S(1)}, u32[]{:S(2)}, u32[]{:S(2)}) collective-permute-start(f32[35,66,1]{1,2,0:T(1,128)S(1)} %copy.45), channel_id=1, source_target_pairs={{1,0},{2,1},{3,2},{4,3},{5,4},{6,5},{7,6},{8,7},{9,8},{10,9},{11,1... | collective-permute-start | bytes 27728 | tf_op jit(solution)/shard_map/ppermute | solution.py:37
  (20 other events, 34.3 us)
Sparse Core Ops, SparseCore 0:
  15.2 50.6 all-reduce.2
